TPU v7x, 256 devices: a whole 4x4x8 slice. The times are simulated.
256 devices in a mesh: snap: 8 (over y, core), vtx: 32 (over z, x).
Axes of the slice: x: 4, y: 4, z: 8, core: 2. Of those that a mesh axis runs over, the one named last changes fastest.
Arguments:
- features: bfloat16 [16, 32768, 128], P('snap', 'vtx'), may hold values from -6 to 6
- tile_vals: bfloat16 [16, 256, 16, 128, 128], P('snap', 'vtx'), may hold values from -0.25 to 0.25
- tile_cols: int32 [16, 256, 16], P('snap', 'vtx'), may hold values from 0 to 255, as said below
- tile_count: int32 [16, 256], P('snap', 'vtx'), may hold values from 1 to 16
- gcn_weight: bfloat16 [128, 128], replicated, may hold values from -0.5 to 0.5
- gcn_bias: float32 [128], replicated, may hold values from -3 to 3
- input_weight: bfloat16 [128, 512], replicated, may hold values from -0.5 to 0.5
- recur_weight: bfloat16 [128, 512], replicated, may hold values from -0.5 to 0.5
- lstm_bias: float32 [512], replicated, may hold values from -4 to 4
- hidden_grad: bfloat16 [32, 1024, 16, 128], P('vtx', 'snap'), may hold values from -6 to 6
Outputs:
- hidden_states: bfloat16 [32, 1024, 16, 128], P('vtx', 'snap')
- grad_gcn_weight: float32 [128, 128], replicated
- grad_gcn_bias: float32 [128], replicated
- grad_input_weight: float32 [128, 512], replicated
- grad_recur_weight: float32 [128, 512], replicated
- grad_lstm_bias: float32 [512], replicated
Inputs may be any that keep to these rules, and one draw needn't show every extreme that they name: `tile_cols`: within one snapshot, the 16 slots of one row block name distinct column blocks, and all slots, live or not, of the row blocks j * 8 to (j + 1) * 8 - 1 together name at most one block of each group of 8 consecutive blocks.
All inputs are finite; a program needn't handle non-finite values.
Results may differ from a plain program's by a relative error of at most 0.0085.
Values may be sent and summed in bfloat16 or wider, within the bound.
No kernel may reach another device: no remote copies, remote signals or barrier semaphores. Data moves between devices by JAX's collectives and lax.ppermute only.
A program may use at most 128 MiB of HBM per device.

v0:
```python
import jax
import jax.numpy as jnp
from jax import lax
from jax.sharding import PartitionSpec as P


def silu_slope(grad_layer, pre_act):
    squeeze = jax.nn.sigmoid(pre_act)
    return (grad_layer.astype(jnp.float32) * squeeze * (1.0 + pre_act * (1.0 - squeeze))).astype(
        jnp.bfloat16
    )


def on_device(
    features,
    tile_vals,
    tile_cols,
    tile_count,
    gcn_weight,
    gcn_bias,
    input_weight,
    recur_weight,
    lstm_bias,
    hidden_grad,
):
    steps_dev, local_verts, feat_width = features.shape
    tile_size = tile_vals.shape[3]
    hidden_size = recur_weight.shape[0]
    live_mask = lax.broadcasted_iota(jnp.int32, tile_cols.shape, 2) < tile_count[:, :, None]
    snap_iota = lax.broadcasted_iota(jnp.int32, tile_cols.shape, 0)
    gathered = lax.all_gather(features, "vtx", axis=1, tiled=True)
    whole_blocks = gathered.reshape(steps_dev, -1, tile_size, feat_width)
    fetched_blocks = whole_blocks[snap_iota, tile_cols]
    blocks_used = jnp.where(
        live_mask[..., None, None], fetched_blocks, jnp.zeros_like(fetched_blocks)
    )
    summed = jnp.einsum(
        "svmij,svmjf->svif", tile_vals, blocks_used, preferred_element_type=jnp.float32
    )
    aggregated = summed.astype(jnp.bfloat16).reshape(steps_dev * local_verts, feat_width)
    pre_act = jnp.dot(aggregated, gcn_weight, preferred_element_type=jnp.float32) + gcn_bias
    layer_out = (
        jax.nn.silu(pre_act).astype(jnp.bfloat16).reshape(steps_dev, local_verts, feat_width)
    )
    vertex_inputs = lax.all_to_all(layer_out, "snap", split_axis=1, concat_axis=0, tiled=True)
    total_steps, vertex_rows, _ = vertex_inputs.shape
    flat_inputs = vertex_inputs.reshape(total_steps * vertex_rows, feat_width)
    input_gates = (
        jnp.dot(flat_inputs, input_weight, preferred_element_type=jnp.float32) + lstm_bias
    ).reshape(total_steps, vertex_rows, 4 * hidden_size)

    def advance(carried, gates_step):
        cell_state, last_out = carried
        pre_gates = gates_step + jnp.dot(last_out, recur_weight, preferred_element_type=jnp.float32)
        gate_in = jax.nn.sigmoid(pre_gates[:, :hidden_size])
        gate_keep = jax.nn.sigmoid(pre_gates[:, hidden_size : 2 * hidden_size])
        gate_new = jnp.tanh(pre_gates[:, 2 * hidden_size : 3 * hidden_size])
        gate_out = jax.nn.sigmoid(pre_gates[:, 3 * hidden_size :])
        cell_state = gate_keep * cell_state + gate_in * gate_new
        new_out = (gate_out * jnp.tanh(cell_state)).astype(jnp.bfloat16)
        return ((cell_state, new_out), (pre_gates, cell_state, new_out))

    zero_cell = jnp.zeros((vertex_rows, hidden_size), jnp.float32)
    start = (zero_cell, jnp.zeros((vertex_rows, hidden_size), jnp.bfloat16))
    _, (all_pre, all_cells, all_outs) = lax.scan(advance, start, input_gates)
    prev_cells = jnp.concatenate([zero_cell[None], all_cells[:-1]], axis=0)
    prev_outs = jnp.concatenate([start[1][None], all_outs[:-1]], axis=0)
    grad_outs = jnp.transpose(hidden_grad[0], (1, 0, 2)).astype(jnp.float32)

    def retreat(carried, step_items):
        grad_cell, grad_back = carried
        pre_gates, cell_state, prev_cell, grad_out = step_items
        gate_in = jax.nn.sigmoid(pre_gates[:, :hidden_size])
        gate_keep = jax.nn.sigmoid(pre_gates[:, hidden_size : 2 * hidden_size])
        gate_new = jnp.tanh(pre_gates[:, 2 * hidden_size : 3 * hidden_size])
        gate_out = jax.nn.sigmoid(pre_gates[:, 3 * hidden_size :])
        squash = jnp.tanh(cell_state)
        grad_total = grad_out + grad_back
        grad_cell = grad_cell + grad_total * gate_out * (1.0 - squash * squash)
        grad_gates = jnp.concatenate(
            [
                grad_cell * gate_new * gate_in * (1.0 - gate_in),
                grad_cell * prev_cell * gate_keep * (1.0 - gate_keep),
                grad_cell * gate_in * (1.0 - gate_new * gate_new),
                grad_total * squash * gate_out * (1.0 - gate_out),
            ],
            axis=1,
        ).astype(jnp.bfloat16)
        grad_back = jnp.einsum(
            "rg,hg->rh", grad_gates, recur_weight, preferred_element_type=jnp.float32
        )
        return ((grad_cell * gate_keep, grad_back), grad_gates)

    _, all_grad_gates = lax.scan(
        retreat, (zero_cell, zero_cell), (all_pre, all_cells, prev_cells, grad_outs), reverse=True
    )
    flat_gates = all_grad_gates.reshape(total_steps * vertex_rows, 4 * hidden_size)
    grad_input = jnp.einsum(
        "rf,rg->fg", flat_inputs, flat_gates, preferred_element_type=jnp.float32
    )
    grad_recur = jnp.einsum(
        "rh,rg->hg",
        prev_outs.reshape(total_steps * vertex_rows, hidden_size),
        flat_gates,
        preferred_element_type=jnp.float32,
    )
    grad_bias = jnp.sum(flat_gates.astype(jnp.float32), axis=0)
    grad_layer = jnp.einsum(
        "rg,fg->rf", flat_gates, input_weight, preferred_element_type=jnp.float32
    ).astype(jnp.bfloat16)
    grad_snap = lax.all_to_all(
        grad_layer.reshape(total_steps, vertex_rows, feat_width),
        "snap",
        split_axis=0,
        concat_axis=1,
        tiled=True,
    )
    grad_snap = grad_snap.reshape(steps_dev * local_verts, feat_width)
    grad_pre = silu_slope(grad_snap, pre_act)
    grad_gcn = jnp.einsum("rf,rg->fg", aggregated, grad_pre, preferred_element_type=jnp.float32)
    grad_gbias = jnp.sum(grad_pre.astype(jnp.float32), axis=0)
    grad_gcn, grad_gbias, grad_input, grad_recur, grad_bias = lax.psum(
        (grad_gcn, grad_gbias, grad_input, grad_recur, grad_bias), ("snap", "vtx")
    )
    hidden_states = jnp.transpose(all_outs, (1, 0, 2))[None]
    return (hidden_states, grad_gcn, grad_gbias, grad_input, grad_recur, grad_bias)


def solution(mesh):
    return jax.shard_map(
        on_device,
        mesh=mesh,
        in_specs=(
            P("snap", "vtx", None),
            P("snap", "vtx", None, None, None),
            P("snap", "vtx", None),
            P("snap", "vtx"),
            P(),
            P(),
            P(),
            P(),
            P(),
            P("vtx", "snap", None, None),
        ),
        out_specs=(P("vtx", "snap", None, None), P(), P(), P(), P(), P()),
        check_vma=False,
    )
```

profile of v0, /device:TPU:1, one launch (start us, length us, event | category | flops | bytes accessed | tf_op | source)
XLA Modules:
  0.0 570.2 jit_solution(6579747021246747212)
XLA Ops:
  9.5 145.1 %all-gather.2.cloned.1.call-done = bf16[2,32768,128]{2,1,0:T(8,128)(2,1)} async-done(((bf16[2,1024,128]{2,1,0:T(8,128)(2,1)}), bf16[2,32768,128]{2,1,0:T(8,128)(2,1)}) %all-gather.2.cloned.1.call-update) | async-done | bytes 16777232 | tf_op jit(solution)/shard_map/all_gather | solution.py:31
  154.6 15.9 %gather_fusion = bf16[256,128,128]{2,1,0:T(8,128)(2,1)} fusion(bf16[2,256,128,128]{3,2,1,0:T(8,128)(2,1)} %bitcast.136, s32[256]{0:T(256)S(1)} %reshape.144), kind=kCustom, calls=%fused_computation | custom fusion | bytes 16779264 | tf_op jit(solution)/shard_map/gather | solution.py:33
  170.4 8.2 %fusion.53 = bf16[2,8,128,128]{2,3,1,0:T(8,128)(2,1)S(1)} fusion(bf16[2,8,16,128,128]{4,3,2,1,0:T(8,128)(2,1)} %param.15, bf16[2,8,16,128,128]{4,3,2,1,0:T(8,128)(2,1)} %bitcast.132, pred[2,8,16]{2,1,0:T(8,128)(4,1)S(1)} %iota_compare_fusion), kind=kOutput, calls=%fused_computation.77 | convolution fusion | flops 1078198272 | bytes 17301760 | tf_op jit(solution)/shard_map/svmij,svmjf->svif/dot_general | solution.py:37
  179.4 1.4 multiply_convert_fusion.2
  180.8 1.3 copy.28
  182.2 5.3 all-to-all-start
  187.5 1.1 convert_bitcast_fusion.1
  188.6 8.3 %all-to-all-done = bf16[2,1024,128]{2,0,1:T(2,128)(2,1)S(1)} async-done(((bf16[2,1024,128]{2,0,1:T(2,128)(2,1)}), bf16[2,1024,128]{2,0,1:T(2,128)(2,1)S(1)}, u32[]{:S(2)}, u32[]{:S(2)}) %all-to-all-start) | async-done | bytes 524320 | tf_op jit(solution)/shard_map/all_to_all | solution.py:45
  197.1 2.6 convolution_add_fusion.1
  199.7 41.2 %while.38 = (s32[]{:T(128)}, f32[128,128]{1,0:T(8,128)S(1)}, bf16[128,128]{1,0:T(8,128)(2,1)S(1)}, f32[16,128,512]{2,1,0:T(8,128)}, f32[16,128,128]{2,1,0:T(8,12...) while((s32[]{:T(128)}, f32[128,128]{1,0:T(8,128)S(1)}, ...), condition=%wide.region_1.2_spmd.clone, body=%wide.region_0.1_spmd.clone.sunk | while | flops 17104900 | bytes 1541236 | solution.py:65
  199.7 1.9 bitcast_dynamic-update-slice_fusion.6
  202.3 1.8 bitcast_dynamic-update-slice_fusion.6
  204.9 1.9 bitcast_dynamic-update-slice_fusion.6
  207.5 1.8 bitcast_dynamic-update-slice_fusion.6
  210.0 1.8 bitcast_dynamic-update-slice_fusion.6
  212.6 1.8 bitcast_dynamic-update-slice_fusion.6
  215.2 1.8 bitcast_dynamic-update-slice_fusion.6
  217.7 1.8 bitcast_dynamic-update-slice_fusion.6
  220.3 1.9 bitcast_dynamic-update-slice_fusion.6
  222.9 1.8 bitcast_dynamic-update-slice_fusion.6
  225.5 1.8 bitcast_dynamic-update-slice_fusion.6
  228.0 1.8 bitcast_dynamic-update-slice_fusion.6
  230.6 1.8 bitcast_dynamic-update-slice_fusion.6
  233.2 1.8 bitcast_dynamic-update-slice_fusion.6
  235.7 1.9 bitcast_dynamic-update-slice_fusion.6
  238.3 1.9 bitcast_dynamic-update-slice_fusion.6
  241.0 1.3 concatenate.44
  242.5 49.4 %while.39 = (s32[]{:T(128)}, f32[128,128]{1,0:T(8,128)S(1)}, f32[128,128]{1,0:T(8,128)S(1)}, bf16[16,128,512]{2,1,0:T(8,128)(2,1)S(1)}, f32[16,128,128]{2,1,0:T(...) while((s32[]{:T(128)}, f32[128,128]{1,0:T(8,128)S(1)}, ...), condition=%wide.region_3.4_spmd.clone, body=%wide.region_2.3_spmd.clone.sunk | while | flops 18481156 | bytes 2162843 | solution.py:94
  242.5 1.0 dynamic-slice_bitcast_fusion.2
  243.5 1.0 multiply_convert_fusion.4
  245.6 1.0 dynamic-slice_bitcast_fusion.2
  246.6 1.0 multiply_convert_fusion.4
  248.7 1.0 dynamic-slice_bitcast_fusion.2
  249.6 1.0 multiply_convert_fusion.4
  251.8 1.0 dynamic-slice_bitcast_fusion.2
  252.7 1.0 multiply_convert_fusion.4
  254.8 1.0 dynamic-slice_bitcast_fusion.2
  255.8 1.0 multiply_convert_fusion.4
  257.9 1.0 dynamic-slice_bitcast_fusion.2
  258.9 1.0 multiply_convert_fusion.4
  261.0 1.0 dynamic-slice_bitcast_fusion.2
  264.1 1.0 dynamic-slice_bitcast_fusion.2
  267.2 1.0 dynamic-slice_bitcast_fusion.2
  270.3 1.0 dynamic-slice_bitcast_fusion.2
  273.4 1.0 dynamic-slice_bitcast_fusion.2
  276.5 1.0 dynamic-slice_bitcast_fusion.2
  279.6 1.0 dynamic-slice_bitcast_fusion.2
  282.7 1.0 dynamic-slice_bitcast_fusion.2
  285.8 1.0 dynamic-slice_bitcast_fusion.2
  288.8 1.0 dynamic-slice_bitcast_fusion.2
  291.9 2.1 copy.34
  294.0 1.5 convolution_convert_fusion
  295.5 4.3 all-to-all-start.1
  299.8 2.2 convolution_bitcast_fusion
  302.0 1.2 fusion.69
  303.1 6.1 %all-to-all-done.1 = bf16[16,128,128]{2,1,0:T(8,128)(2,1)S(1)} async-done(((bf16[16,128,128]{2,1,0:T(8,128)(2,1)}), bf16[16,128,128]{2,1,0:T(8,128)(2,1)S(1)}, u32[]{:S(2)}, u32[]{:S(2)}) %all-to-all-start.1) | async-done | bytes 524320 | tf_op jit(solution)/shard_map/all_to_all | solution.py:111
  309.5 1.0 copy-done.4
  311.0 1.0 fusion.68
  312.0 1.1 copy.38
  313.4 73.9 %all-reduce.2 = (f32[128]{0:T(128)}, f32[512]{0:T(512)}) all-reduce(f32[128]{0:T(128)S(1)} %get-tuple-element.334, f32[512]{0:T(512)S(1)} %convert_reduce_fusion), channel_id=1, replica_groups=mesh['snap'=8,'vtx'=32] {'snap','vtx'}, use_global_device_ids=true, to_apply=%region_6.7 | all-reduce | flops 640 | bytes 5120 | tf_op jit(solution)/shard_map/psum | solution.py:122
  387.4 171.2 %all-reduce.6.cloned.1.call-done = (f32[128,128]{1,0:T(8,128)}, f32[128,512]{1,0:T(8,128)}, f32[128,512]{1,0:T(8,128)}) async-done(((f32[128,128]{1,0:T(8,128)}, f32[128,512]{1,0:T(8,128)}, f32[128,512]{1,0:T(8,128)}), (f32[128,128]{1,0:T(8,128)}, f32[128,512]{1,0:T(8,128)}, f32[128,512]{1,0:T(8,128)})) %all-reduce.6.cloned.1.call-update) | async-done | bytes 589840 | tf_op jit(solution)/shard_map/psum | solution.py:122
  558.6 1.5 copy.76
  560.0 1.7 copy.77
  561.7 1.7 copy.78
  (133 shorter events, 43.2 us)
Async XLA Ops:
  7.2 189.9 %copy-start = (bf16[128,512]{1,0:T(8,128)(2,1)S(1)}, bf16[128,512]{1,0:T(8,128)(2,1)}, u32[]{:S(2)}) copy-start(bf16[128,512]{1,0:T(8,128)(2,1)} %param.20) | copy-start | bytes 393220
  7.2 147.4 %all-gather.2.cloned.1.call-start = ((), (), s32[]{:S(2)}) async-start(), calls=%async_computation.2 | async-start | bytes 17301504 | tf_op jit(solution)/shard_map/all_gather | solution.py:31
  170.4 9.0 %copy-start.9 = (bf16[128,128]{1,0:T(8,128)(2,1)S(1)}, bf16[128,128]{1,0:T(8,128)(2,1)}, u32[]{:S(2)}) copy-start(bf16[128,128]{1,0:T(8,128)(2,1)} %param.18) | copy-start | bytes 98308
  170.4 9.0 %copy-start.10 = (f32[128]{0:T(128)S(1)}, f32[128]{0:T(128)}, u32[]{:S(2)}) copy-start(f32[128]{0:T(128)} %param.19) | copy-start | bytes 1540
  178.6 0.8 copy-start.6
  178.6 8.9 %copy-start.5 = (bf16[1,128,16,128]{3,2,1,0:T(8,128)(2,1)S(1)}, bf16[1,128,16,128]{3,2,1,0:T(8,128)(2,1)}, u32[]{:S(2)}) copy-start(bf16[1,128,16,128]{3,2,1,0:T(8,128)(2,1)} %param.23) | copy-start | bytes 1572868
  180.8 16.3 %copy-start.8 = (f32[512]{0:T(512)S(1)}, f32[512]{0:T(512)}, u32[]{:S(2)}) copy-start(f32[512]{0:T(512)} %param.22) | copy-start | bytes 6148
  182.2 14.8 %all-to-all-start = ((bf16[2,1024,128]{2,0,1:T(2,128)(2,1)}), bf16[2,1024,128]{2,0,1:T(2,128)(2,1)S(1)}, u32[]{:S(2)}, u32[]{:S(2)}) async-start(bf16[2,1024,128]{2,0,1:T(2,128)(2,1)} %copy.28), calls=%async_computation | async-start | bytes 1048576 | tf_op jit(solution)/shard_map/all_to_all | solution.py:45
  187.5 12.2 %copy-start.1 = (bf16[128,512]{1,0:T(8,128)(2,1)S(1)}, bf16[128,512]{1,0:T(8,128)(2,1)}, u32[]{:S(2)}) copy-start(bf16[128,512]{1,0:T(8,128)(2,1)} %param.21) | copy-start | bytes 393220
  240.9 1.3 copy-start.3
  295.5 13.8 %all-to-all-start.1 = ((bf16[16,128,128]{2,1,0:T(8,128)(2,1)}), bf16[16,128,128]{2,1,0:T(8,128)(2,1)S(1)}, u32[]{:S(2)}, u32[]{:S(2)}) async-start(bf16[16,128,128]{2,1,0:T(8,128)(2,1)} %bitcast.143), calls=%async_computation.1 | async-start | bytes 1048576 | tf_op jit(solution)/shard_map/all_to_all | solution.py:111
  299.8 258.8 %all-reduce.6.cloned.1.call-start = ((), (), s32[]{:S(2)}) async-start(), calls=%async_computation.3 | async-start | bytes 1179648 | tf_op jit(solution)/shard_map/psum | solution.py:122
  303.1 8.8 %copy-start.2 = (bf16[16,128,128]{2,1,0:T(8,128)(2,1)S(1)}, bf16[16,128,128]{2,1,0:T(8,128)(2,1)}, u32[]{:S(2)}) copy-start(bf16[16,128,128]{2,1,0:T(8,128)(2,1)} %get-tuple-element.229) | copy-start | bytes 1572868
  309.3 1.2 copy-start.4
  309.3 1.7 copy-start.7
Sparse Core Ops, SparseCore 0:
  10.6 143.9 all-gather.1
  312.1 246.4 all-reduce.5
where the time goes:
time: 573 us; the launch traced here: 570 us
  waiting for transfers between devices  331 us (58%)
  blocking collectives  73.9 us (13%)
  matrix products  50.5 us (9%)
  other arithmetic  44.9 us (8%)
  local copies, waits for them, and re-layouts  44.5 us (8%)
  between operations  14.2 us (2%)
  starting transfers between devices  9.64 us (2%)
    psum x1, waiting for transfers between devices, on_device(): lax.psum((grad_gcn, grad_gbias, grad_input, grad_recur, grad_bias), ('sna...  171 us
    all_gather x1, waiting for transfers between devices, on_device(): gathered = lax.all_gather(features, 'vtx', axis=1, tiled=True)  145 us
    psum x1, blocking collectives, on_device(): lax.psum((grad_gcn, grad_gbias, grad_input, grad_recur, grad_bias), ('sna...  73.9 us
    another operation x32, other arithmetic  29.8 us
    dot_general x16, matrix products, advance(): jnp.dot(last_out, recur_weight, preferred_element_type=jnp.float32)  29.5 us
    gather x1, local copies, waits for them, and re-layouts, on_device(): fetched_blocks = whole_blocks[snap_iota, tile_cols]  15.9 us
    squeeze x16, local copies, waits for them, and re-layouts, on_device(): _, (all_pre, all_cells, all_outs) = lax.scan(advance, start, input_gates)  15.6 us
  transfers between devices with their start and end apart: 4, of which 4 were waited for; matrix products, arithmetic and copies ran while one was open for 1% of the time, Pallas kernels for 0%

commit v1 on v0

--- a/solution.py
+++ b/solution.py
@@ -2,6 +2,11 @@
 import jax.numpy as jnp
 from jax import lax
 from jax.sharding import PartitionSpec as P
+
+
+def by_each_axis(x, one, other):
+    inner = lax.psum(x, one)
+    return lax.psum(inner, other)
 
 
 def silu_slope(grad_layer, pre_act):
@@ -119,8 +124,8 @@
     grad_pre = silu_slope(grad_snap, pre_act)
     grad_gcn = jnp.einsum("rf,rg->fg", aggregated, grad_pre, preferred_element_type=jnp.float32)
     grad_gbias = jnp.sum(grad_pre.astype(jnp.float32), axis=0)
-    grad_gcn, grad_gbias, grad_input, grad_recur, grad_bias = lax.psum(
-        (grad_gcn, grad_gbias, grad_input, grad_recur, grad_bias), ("snap", "vtx")
+    grad_gcn, grad_gbias, grad_input, grad_recur, grad_bias = by_each_axis(
+        (grad_gcn, grad_gbias, grad_input, grad_recur, grad_bias), "snap", "vtx"
     )
     hidden_states = jnp.transpose(all_outs, (1, 0, 2))[None]
     return (hidden_states, grad_gcn, grad_gbias, grad_input, grad_recur, grad_bias)

time: 573 us -> 550 us (0.960)
  waiting for transfers between devices: 331 us -> 291 us
  local copies, waits for them, and re-layouts: 44.5 us -> 55.5 us
    psum x1 -> x2, waiting for transfers between devices: 171 us -> 131 us  [the longest x1 70.7 us: by_each_axis(): return lax.psum(inner, other)]
    dynamic_update_slice x16, local copies, waits for them, and re-layouts: 0.13 us -> 10 us  [on_device(): _, (all_pre, all_cells, all_outs) = lax.scan(advance, start, input_gates)]
    psum x1 -> x2, blocking collectives: 73.9 us -> 75.9 us  [the longest x1 61.5 us: by_each_axis(): return lax.psum(inner, other)]
  transfers between devices with their start and end apart: 4 -> 5, of which waited for: 4 -> 5; matrix products, arithmetic and copies ran while one was open for 1% -> 1% of each run, Pallas kernels for 0% -> 0%
where the time goes in v1:
time: 550 us; the launch traced here: 543 us
  waiting for transfers between devices  291 us (53%)
  blocking collectives  75.9 us (14%)
  local copies, waits for them, and re-layouts  55.5 us (10%)
  matrix products  51.4 us (9%)
  other arithmetic  44.9 us (8%)
  between operations  13.9 us (3%)
  starting transfers between devices  9.66 us (2%)
    all_gather x1, waiting for transfers between devices, on_device(): gathered = lax.all_gather(features, 'vtx', axis=1, tiled=True)  145 us
    psum x1, waiting for transfers between devices, by_each_axis(): return lax.psum(inner, other)  70.7 us
    psum x1, blocking collectives, by_each_axis(): return lax.psum(inner, other)  61.5 us
    psum x1, waiting for transfers between devices, by_each_axis(): inner = lax.psum(x, one)  59.9 us
    another operation x32, other arithmetic  29.8 us
    dot_general x16, matrix products, advance(): jnp.dot(last_out, recur_weight, preferred_element_type=jnp.float32)  29.4 us
    gather x1, local copies, waits for them, and re-layouts, on_device(): fetched_blocks = whole_blocks[snap_iota, tile_cols]  15.9 us
    squeeze x16, local copies, waits for them, and re-layouts, on_device(): _, (all_pre, all_cells, all_outs) = lax.scan(advance, start, input_gates)  15.6 us
  transfers between devices with their start and end apart: 5, of which 5 were waited for; matrix products, arithmetic and copies ran while one was open for 1% of the time, Pallas kernels for 0%

profile of v1, /device:TPU:1, one launch (start us, length us, event | category | flops | bytes accessed | tf_op | source)
XLA Modules:
  0.0 543.0 jit_solution(6394655240976964662)
XLA Ops:
  9.5 145.1 %all-gather.2.cloned.1.call-done = bf16[2,32768,128]{2,1,0:T(8,128)(2,1)} async-done(((bf16[2,1024,128]{2,1,0:T(8,128)(2,1)}), bf16[2,32768,128]{2,1,0:T(8,128)(2,1)}) %all-gather.2.cloned.1.call-update) | async-done | bytes 16777232 | tf_op jit(solution)/shard_map/all_gather | solution.py:36
  154.6 15.9 %gather_fusion = bf16[256,128,128]{2,1,0:T(8,128)(2,1)} fusion(bf16[2,256,128,128]{3,2,1,0:T(8,128)(2,1)} %bitcast.136, s32[256]{0:T(256)S(1)} %reshape.144), kind=kCustom, calls=%fused_computation | custom fusion | bytes 16779264 | tf_op jit(solution)/shard_map/gather | solution.py:38
  170.4 8.2 %fusion.53 = bf16[2,8,128,128]{2,3,1,0:T(8,128)(2,1)S(1)} fusion(bf16[2,8,16,128,128]{4,3,2,1,0:T(8,128)(2,1)} %param.15, bf16[2,8,16,128,128]{4,3,2,1,0:T(8,128)(2,1)} %bitcast.132, pred[2,8,16]{2,1,0:T(8,128)(4,1)S(1)} %iota_compare_fusion), kind=kOutput, calls=%fused_computation.77 | convolution fusion | flops 1078198272 | bytes 17301760 | tf_op jit(solution)/shard_map/svmij,svmjf->svif/dot_general | solution.py:42
  179.4 1.4 multiply_convert_fusion.2
  180.8 1.3 copy.28
  182.2 5.3 all-to-all-start
  187.5 1.1 convert_bitcast_fusion.1
  188.6 8.3 %all-to-all-done = bf16[2,1024,128]{2,0,1:T(2,128)(2,1)S(1)} async-done(((bf16[2,1024,128]{2,0,1:T(2,128)(2,1)}), bf16[2,1024,128]{2,0,1:T(2,128)(2,1)S(1)}, u32[]{:S(2)}, u32[]{:S(2)}) %all-to-all-start) | async-done | bytes 524320 | tf_op jit(solution)/shard_map/all_to_all | solution.py:50
  197.1 2.7 convolution_add_fusion.1
  199.8 50.6 %while.38 = (s32[]{:T(128)}, f32[128,128]{1,0:T(8,128)S(1)}, bf16[128,128]{1,0:T(8,128)(2,1)S(1)}, f32[16,128,512]{2,1,0:T(8,128)}, f32[16,128,128]{2,1,0:T(8,12...) while((s32[]{:T(128)}, f32[128,128]{1,0:T(8,128)S(1)}, ...), condition=%wide.region_1.2_spmd.clone, body=%wide.region_0.1_spmd.clone.sunk | while | flops 17104900 | bytes 1541744 | solution.py:70
  199.8 1.8 bitcast_dynamic-update-slice_fusion.6
  202.9 1.8 bitcast_dynamic-update-slice_fusion.6
  206.1 1.8 bitcast_dynamic-update-slice_fusion.6
  209.2 1.8 bitcast_dynamic-update-slice_fusion.6
  212.4 1.9 bitcast_dynamic-update-slice_fusion.6
  215.6 1.8 bitcast_dynamic-update-slice_fusion.6
  218.8 1.8 bitcast_dynamic-update-slice_fusion.6
  221.9 1.8 bitcast_dynamic-update-slice_fusion.6
  225.1 1.8 bitcast_dynamic-update-slice_fusion.6
  228.3 1.8 bitcast_dynamic-update-slice_fusion.6
  231.4 1.8 bitcast_dynamic-update-slice_fusion.6
  234.6 1.8 bitcast_dynamic-update-slice_fusion.6
  237.8 1.8 bitcast_dynamic-update-slice_fusion.6
  240.9 1.8 bitcast_dynamic-update-slice_fusion.6
  244.1 1.9 bitcast_dynamic-update-slice_fusion.6
  247.2 1.8 bitcast_dynamic-update-slice_fusion.6
  250.4 1.3 slice.54
  251.7 1.1 concatenate.44
  253.0 49.4 %while.39 = (s32[]{:T(128)}, f32[128,128]{1,0:T(8,128)S(1)}, f32[128,128]{1,0:T(8,128)S(1)}, bf16[16,128,512]{2,1,0:T(8,128)(2,1)S(1)}, f32[16,128,128]{2,1,0:T(...) while((s32[]{:T(128)}, f32[128,128]{1,0:T(8,128)S(1)}, ...), condition=%wide.region_3.4_spmd.clone, body=%wide.region_2.3_spmd.clone.sunk | while | flops 18481156 | bytes 2162843 | solution.py:99
  253.0 1.0 dynamic-slice_bitcast_fusion.2
  254.0 1.0 multiply_convert_fusion.4
  256.1 1.0 dynamic-slice_bitcast_fusion.2
  259.2 1.0 dynamic-slice_bitcast_fusion.2
  262.3 1.0 dynamic-slice_bitcast_fusion.2
  265.4 1.0 dynamic-slice_bitcast_fusion.2
  268.5 1.0 dynamic-slice_bitcast_fusion.2
  271.6 1.0 dynamic-slice_bitcast_fusion.2
  274.7 1.0 dynamic-slice_bitcast_fusion.2
  277.7 1.0 dynamic-slice_bitcast_fusion.2
  280.8 1.0 dynamic-slice_bitcast_fusion.2
  283.9 1.0 dynamic-slice_bitcast_fusion.2
  287.0 1.0 dynamic-slice_bitcast_fusion.2
  288.0 1.0 multiply_convert_fusion.4
  290.1 1.0 dynamic-slice_bitcast_fusion.2
  293.2 1.0 dynamic-slice_bitcast_fusion.2
  296.3 1.0 dynamic-slice_bitcast_fusion.2
  297.3 1.0 multiply_convert_fusion.4
  299.4 1.0 dynamic-slice_bitcast_fusion.2
  302.5 2.1 copy.34
  304.5 1.5 convolution_convert_fusion
  306.0 4.3 all-to-all-start.1
  310.3 2.2 convolution_bitcast_fusion
  312.5 1.2 fusion.69
  313.6 6.1 %all-to-all-done.1 = bf16[16,128,128]{2,1,0:T(8,128)(2,1)S(1)} async-done(((bf16[16,128,128]{2,1,0:T(8,128)(2,1)}), bf16[16,128,128]{2,1,0:T(8,128)(2,1)S(1)}, u32[]{:S(2)}, u32[]{:S(2)}) %all-to-all-start.1) | async-done | bytes 524320 | tf_op jit(solution)/shard_map/all_to_all | solution.py:116
  320.0 1.0 copy-done.3
  321.5 2.0 fusion.68
  323.6 59.9 %all-reduce.11.cloned.1.call-done = (f32[128,128]{1,0:T(8,128)}, f32[128,512]{1,0:T(8,128)}, f32[128,512]{1,0:T(8,128)}) async-done(((f32[128,128]{1,0:T(8,128)}, f32[128,512]{1,0:T(8,128)}, f32[128,512]{1,0:T(8,128)}), (f32[128,128]{1,0:T(8,128)}, f32[128,512]{1,0:T(8,128)}, f32[128,512]{1,0:T(8,128)})) %all-reduce.11.cloned.1.call-update) | async-done | bytes 589840 | tf_op jit(solution)/shard_map/psum | solution.py:8
  383.5 1.1 copy.38
  385.0 14.4 %all-reduce.4 = (f32[128]{0:T(128)S(1)}, f32[512]{0:T(512)S(1)}) all-reduce(f32[128]{0:T(128)S(1)} %get-tuple-element.339, f32[512]{0:T(512)S(1)} %convert_reduce_fusion), channel_id=1, replica_groups=mesh['snap'=8,'vtx'=32] {'snap'}, use_global_device_ids=true, to_apply=%region_7.8 | all-reduce | flops 640 | bytes 5120 | tf_op jit(solution)/shard_map/psum | solution.py:8
  399.3 61.5 %all-reduce.2 = (f32[128]{0:T(128)}, f32[512]{0:T(512)}) all-reduce(f32[128]{0:T(128)S(1)} %get-tuple-element.329, f32[512]{0:T(512)S(1)} %get-tuple-element.330), channel_id=1, replica_groups=mesh['snap'=8,'vtx'=32] {'vtx'}, use_global_device_ids=true, to_apply=%region_8.9 | all-reduce | flops 640 | bytes 5120 | tf_op jit(solution)/shard_map/psum | solution.py:9
  460.9 70.7 %all-reduce.9.cloned.1.call-done = (f32[128,128]{1,0:T(8,128)}, f32[128,512]{1,0:T(8,128)}, f32[128,512]{1,0:T(8,128)}) async-done(((f32[128,128]{1,0:T(8,128)}, f32[128,512]{1,0:T(8,128)}, f32[128,512]{1,0:T(8,128)}), (f32[128,128]{1,0:T(8,128)}, f32[128,512]{1,0:T(8,128)}, f32[128,512]{1,0:T(8,128)})) %all-reduce.9.cloned.1.call-update) | async-done | bytes 589840 | tf_op jit(solution)/shard_map/psum | solution.py:9
  531.6 1.5 copy.79
  533.1 1.7 copy.80
  534.8 1.7 copy.81
  (133 shorter events, 56.0 us)
Async XLA Ops:
  7.2 189.9 %copy-start = (bf16[128,512]{1,0:T(8,128)(2,1)S(1)}, bf16[128,512]{1,0:T(8,128)(2,1)}, u32[]{:S(2)}) copy-start(bf16[128,512]{1,0:T(8,128)(2,1)} %param.20) | copy-start | bytes 393220
  7.2 147.4 %all-gather.2.cloned.1.call-start = ((), (), s32[]{:S(2)}) async-start(), calls=%async_computation.2 | async-start | bytes 17301504 | tf_op jit(solution)/shard_map/all_gather | solution.py:36
  170.4 9.0 %copy-start.7 = (bf16[128,128]{1,0:T(8,128)(2,1)S(1)}, bf16[128,128]{1,0:T(8,128)(2,1)}, u32[]{:S(2)}) copy-start(bf16[128,128]{1,0:T(8,128)(2,1)} %param.18) | copy-start | bytes 98308
  170.4 9.0 %copy-start.8 = (f32[128]{0:T(128)S(1)}, f32[128]{0:T(128)}, u32[]{:S(2)}) copy-start(f32[128]{0:T(128)} %param.19) | copy-start | bytes 1540
  178.6 0.8 copy-start.5
  178.6 8.9 %copy-start.4 = (bf16[1,128,16,128]{3,2,1,0:T(8,128)(2,1)S(1)}, bf16[1,128,16,128]{3,2,1,0:T(8,128)(2,1)}, u32[]{:S(2)}) copy-start(bf16[1,128,16,128]{3,2,1,0:T(8,128)(2,1)} %param.23) | copy-start | bytes 1572868
  180.8 16.3 %copy-start.6 = (f32[512]{0:T(512)S(1)}, f32[512]{0:T(512)}, u32[]{:S(2)}) copy-start(f32[512]{0:T(512)} %param.22) | copy-start | bytes 6148
  182.2 14.8 %all-to-all-start = ((bf16[2,1024,128]{2,0,1:T(2,128)(2,1)}), bf16[2,1024,128]{2,0,1:T(2,128)(2,1)S(1)}, u32[]{:S(2)}, u32[]{:S(2)}) async-start(bf16[2,1024,128]{2,0,1:T(2,128)(2,1)} %copy.28), calls=%async_computation | async-start | bytes 1048576 | tf_op jit(solution)/shard_map/all_to_all | solution.py:50
  187.5 12.3 %copy-start.1 = (bf16[128,512]{1,0:T(8,128)(2,1)S(1)}, bf16[128,512]{1,0:T(8,128)(2,1)}, u32[]{:S(2)}) copy-start(bf16[128,512]{1,0:T(8,128)(2,1)} %param.21) | copy-start | bytes 393220
  306.0 13.8 %all-to-all-start.1 = ((bf16[16,128,128]{2,1,0:T(8,128)(2,1)}), bf16[16,128,128]{2,1,0:T(8,128)(2,1)S(1)}, u32[]{:S(2)}, u32[]{:S(2)}) async-start(bf16[16,128,128]{2,1,0:T(8,128)(2,1)} %bitcast.143), calls=%async_computation.1 | async-start | bytes 1048576 | tf_op jit(solution)/shard_map/all_to_all | solution.py:116
  310.3 73.2 %all-reduce.11.cloned.1.call-start = ((), (), s32[]{:S(2)}) async-start(), calls=%async_computation.4 | async-start | bytes 1179648 | tf_op jit(solution)/shard_map/psum | solution.py:8
  319.8 1.2 copy-start.3
  319.8 63.7 %copy-start.2 = (bf16[16,128,128]{2,1,0:T(8,128)(2,1)S(1)}, bf16[16,128,128]{2,1,0:T(8,128)(2,1)}, u32[]{:S(2)}) copy-start(bf16[16,128,128]{2,1,0:T(8,128)(2,1)} %get-tuple-element.229) | copy-start | bytes 1572868
  323.5 208.1 %all-reduce.9.cloned.1.call-start = ((), (), s32[]{:S(2)}) async-start(), calls=%async_computation.3 | async-start | bytes 1179648 | tf_op jit(solution)/shard_map/psum | solution.py:9
Sparse Core Ops, SparseCore 0:
  10.6 143.9 all-gather.1
  323.6 59.7 all-reduce.10
  387.1 144.4 all-reduce.8
